TPU v7x, 32 devices: a whole 2x2x4 slice. The times are simulated.
32 devices in a mesh: row: 4 (over x, core), col: 8 (over z, y).
Axes of the slice: x: 2, y: 2, z: 4, core: 2. Of those that a mesh axis runs over, the one named last changes fastest.
Arguments:
- w_inter: bfloat16 [3072, 4, 1024], P('col', 'row'), may hold values from -0.109375 to 0.109375
- t_panel: bfloat16 [1024, 4, 3072], P('col', None, 'row'), may hold values from -6 to 6
- amplitudes: float32 [1024, 4, 4, 1024], P('col', None, 'row'), may hold values from -4 to 4
- e_occ: float32 [4], replicated, may hold values from -2 to -0.5
- e_vir: float32 [1024], replicated, may hold values from 0.3 to 3
Outputs:
- new_amplitudes: float32 [1024, 4, 4, 1024], P('col', None, 'row')
All inputs are finite; a program needn't handle non-finite values.
Results may differ from a plain program's by a relative error of at most 0.0003.
Values may be sent and summed in bfloat16 or wider, within the bound.
A program may use at most 64 MiB of HBM per device.

v0:
```python
import jax
import jax.numpy as jnp
from jax import lax
from jax.sharding import PartitionSpec as P


def on_device(w_inter, t_panel, amplitudes, e_occ, e_vir):
    row_index = lax.axis_index("row")
    col_index = lax.axis_index("col")
    occ_dev = w_inter.shape[1]
    vir_all = w_inter.shape[2]
    vir_dev = t_panel.shape[0]
    occ_all = t_panel.shape[1]
    t_full = lax.all_gather(t_panel, "row", axis=2, tiled=True)
    t_matrix = t_full.reshape(vir_dev * occ_all, t_full.shape[2])
    piece = lax.all_gather(w_inter, "col", axis=0, tiled=True)
    row_count = piece.shape[0]
    totals = jnp.dot(
        t_matrix, piece.reshape(row_count, occ_dev * vir_all), preferred_element_type=jnp.float32
    )
    contracted = totals.reshape(vir_dev, occ_all, occ_dev, vir_all)
    moved = lax.all_to_all(
        lax.all_to_all(contracted, "row", split_axis=1, concat_axis=2, tiled=True),
        "col",
        split_axis=3,
        concat_axis=0,
        tiled=True,
    )
    mirrored = jnp.transpose(moved, (3, 2, 1, 0))
    occ_mine = lax.dynamic_slice_in_dim(e_occ, row_index * occ_dev, occ_dev)
    vir_mine = lax.dynamic_slice_in_dim(e_vir, col_index * vir_dev, vir_dev)
    gaps = (
        e_occ[None, :, None, None]
        + occ_mine[None, None, :, None]
        - vir_mine[:, None, None, None]
        - e_vir[None, None, None, :]
    )
    return amplitudes + (contracted + mirrored) / gaps


def solution(mesh):
    return jax.shard_map(
        on_device,
        mesh=mesh,
        in_specs=(
            P("col", "row", None),
            P("col", None, "row"),
            P("col", None, "row", None),
            P(),
            P(),
        ),
        out_specs=P("col", None, "row", None),
        check_vma=False,
    )
```

profile of v0, /device:TPU:11, one launch (start us, length us, event | category | flops | bytes accessed | tf_op | source)
XLA Modules:
  0.0 244.8 jit_solution(9391433714847880570)
XLA Ops:
  6.5 0.0 all-gather.3.cloned.1.call-start
  6.5 2.1 copy.10
  8.6 0.0 all-gather.3.cloned.1.call-update
  8.7 0.0 all-gather.5.cloned.1.call-start
  8.7 0.7 all-gather.5.cloned.1.call-update
  9.4 28.6 %all-gather.3.cloned.1.call-done = bf16[128,4,3072]{2,0,1:T(8,128)(2,1)} async-done(((bf16[128,4,768]{2,0,1:T(8,128)(2,1)}), bf16[128,4,3072]{2,0,1:T(8,128)(2,1)}) %all-gather.3.cloned.1.call-update) | async-done | bytes 3145744 | tf_op jit(solution)/shard_map/all_gather | solution.py:14
  38.1 98.8 %all-gather.5.cloned.1.call-done = bf16[3072,1,1024]{2,0,1:T(8,128)(2,1)} async-done(((bf16[384,1,1024]{2,0,1:T(8,128)(2,1)}), bf16[3072,1,1024]{2,0,1:T(8,128)(2,1)}) %all-gather.5.cloned.1.call-update) | async-done | bytes 6291472 | tf_op jit(solution)/shard_map/all_gather | solution.py:16
  136.9 6.4 %fusion = f32[128,4,1024]{2,0,1:T(8,128)S(1)} fusion(bf16[128,4,3072]{2,0,1:T(8,128)(2,1)} %all-gather.3.cloned.1.call-done, bf16[3072,1,1024]{2,0,1:T(8,128)(2,1)} %all-gather.5.cloned.1.call-done), kind=kOutput, calls=%fused_computation | convolution fusion | flops 3221225472 | bytes 11534336 | tf_op jit(solution)/shard_map/dot_general | solution.py:18
  143.3 0.0 copy-start
  143.3 28.7 %all_to_all.30 = f32[128,4,1,1024]{3,0,2,1:T(8,128)S(1)} all-to-all(f32[128,4,1,1024]{3,0,2,1:T(8,128)S(1)} %bitcast.28), channel_id=1, replica_groups=mesh['row'=4,'col'=8] {'row'}, dimensions={1} | all-to-all | bytes 4194304 | tf_op jit(solution)/shard_map/all_to_all | solution.py:23
  172.0 0.0 copy-done
  172.0 1.8 copy.12
  173.8 0.0 copy-start.2
  173.8 0.0 copy-start.3
  173.8 5.1 %all-to-all-start.1 = ((f32[128,1,4,1024]{0,2,1,3:T(4,128)}), f32[128,1,4,1024]{0,2,1,3:T(4,128)S(1)}, u32[]{:S(2)}, u32[]{:S(2)}) async-start(f32[128,1,4,1024]{0,2,1,3:T(4,128)} %copy.12), calls=%async_computation.1 | async-start | bytes 4194304 | tf_op jit(solution)/shard_map/all_to_all | solution.py:22
  178.9 0.0 copy-done.2
  178.9 0.1 dynamic_slice.7
  179.0 0.0 copy-done.3
  179.0 0.6 dynamic_slice.6
  179.6 0.7 broadcast_add_fusion
  180.3 0.1 broadcast_subtract_fusion
  180.4 45.1 %all-to-all-done.1 = f32[128,1,4,1024]{0,2,1,3:T(4,128)S(1)} async-done(((f32[128,1,4,1024]{0,2,1,3:T(4,128)}), f32[128,1,4,1024]{0,2,1,3:T(4,128)S(1)}, u32[]{:S(2)}, u32[]{:S(2)}) %all-to-all-start.1) | async-done | bytes 2097184 | tf_op jit(solution)/shard_map/all_to_all | solution.py:22
  225.4 2.5 %copy.18 = f32[128,1,4,8,128]{0,3,4,2,1:T(8,128)} copy(f32[128,1,4,8,128]{0,2,4,3,1:T(4,128)S(1)} %bitcast.25) | data formatting | bytes 4194304 | tf_op jit(solution)/shard_map/all_to_all | solution.py:22
  228.0 0.0 copy-start.1
  228.0 2.9 %all_to_all.27 = f32[1024,1,4,128]{0,3,2,1:T(8,128)} reshape(f32[8,128,1,4,128]{1,0,4,3,2:T(8,128)} %bitcast.26) | data formatting | bytes 4194304 | tf_op jit(solution)/shard_map/all_to_all | solution.py:22
  230.8 0.0 copy-done.1
  230.8 3.7 %fusion.3 = f32[128,4,1,1024]{3,0,1,2:T(8,128)S(1)} fusion(f32[1024,1,4,128]{0,3,2,1:T(8,128)} %all_to_all.27, f32[128,4,1024]{2,0,1:T(8,128)S(1)} %copy-done.1, f32[128,4,1,1024]{3,2,1,0:T(1,128)} %param.7, f32[1024]{0:T(1024)S(1)} %copy-done.2, f32[128,4]{0,1:T(4,128)S(1)} %broadcast_subtract_fusion), kind=kLoop, calls=%fused_computation.4 | loop fusion | flops 2097152 | bytes 8394752 | tf_op jit(solution)/shard_map/add | solution.py:38
  234.5 3.5 %copy.15 = f32[128,4,1,1024]{3,2,1,0:T(1,128)} copy(f32[128,4,1,1024]{3,0,1,2:T(8,128)S(1)} %fusion.3) | data formatting | bytes 4194304 | tf_op jit(solution)/shard_map/add | solution.py:38
Async XLA Ops:
  6.5 31.5 %all-gather.3.cloned.1.call-start = ((), (), s32[]{:S(2)}) async-start(), calls=%async_computation.2 | async-start | bytes 3932160 | tf_op jit(solution)/shard_map/all_gather | solution.py:14
  8.7 128.2 %all-gather.5.cloned.1.call-start = ((), (), s32[]{:S(2)}) async-start(), calls=%async_computation.3 | async-start | bytes 7077888 | tf_op jit(solution)/shard_map/all_gather | solution.py:16
  143.3 28.7 %copy-start = (f32[128,4,1024]{2,0,1:T(8,128)}, f32[128,4,1024]{2,0,1:T(8,128)S(1)}, u32[]{:S(2)}) copy-start(f32[128,4,1024]{2,0,1:T(8,128)S(1)} %fusion) | copy-start | bytes 6291460
  173.8 5.1 %copy-start.2 = (f32[1024]{0:T(1024)S(1)}, f32[1024]{0:T(1024)}, u32[]{:S(2)}) copy-start(f32[1024]{0:T(1024)} %param.9) | copy-start | bytes 12292
  173.8 5.2 %copy-start.3 = (f32[4]{0:T(128)S(1)}, f32[4]{0:T(128)}, u32[]{:S(2)}) copy-start(f32[4]{0:T(128)} %param.8) | copy-start | bytes 52
  173.8 51.6 %all-to-all-start.1 = ((f32[128,1,4,1024]{0,2,1,3:T(4,128)}), f32[128,1,4,1024]{0,2,1,3:T(4,128)S(1)}, u32[]{:S(2)}, u32[]{:S(2)}) async-start(f32[128,1,4,1024]{0,2,1,3:T(4,128)} %copy.12), calls=%async_computation.1 | async-start | bytes 4194304 | tf_op jit(solution)/shard_map/all_to_all | solution.py:22
  228.0 2.9 %copy-start.1 = (f32[128,4,1024]{2,0,1:T(8,128)S(1)}, f32[128,4,1024]{2,0,1:T(8,128)}, u32[]{:S(2)}) copy-start(f32[128,4,1024]{2,0,1:T(8,128)} %copy-done) | copy-start | bytes 6291460
Sparse Core Ops, SparseCore 0:
  8.9 29.1 all-gather.2
  40.2 96.5 all-gather.4
where the time goes:
time: 249 us; the launch traced here: 245 us
  waiting for transfers between devices  173 us (69%)
  blocking collectives  28.7 us (12%)
  local copies, waits for them, and re-layouts  13.5 us (5%)
  between operations  13.4 us (5%)
  matrix products  6.44 us (3%)
  starting transfers between devices  5.11 us (2%)
  other arithmetic  4.41 us (2%)
    all_gather x1, waiting for transfers between devices, on_device(): piece = lax.all_gather(w_inter, 'col', axis=0, tiled=True)  98.8 us
    all_to_all x1, waiting for transfers between devices, on_device(): lax.all_to_all(lax.all_to_all(contracted, 'row', split_axis=1, concat_axi...  45.1 us
    all_to_all x1, blocking collectives, on_device(): lax.all_to_all(contracted, 'row', split_axis=1, concat_axis=2, tiled=True)  28.7 us
    all_gather x1, waiting for transfers between devices, on_device(): t_full = lax.all_gather(t_panel, 'row', axis=2, tiled=True)  28.6 us
    dot_general x1, matrix products, on_device(): jnp.dot(t_matrix, piece.reshape(row_count, occ_dev * vir_all), preferred_...  6.44 us
    all_to_all x2, local copies, waits for them, and re-layouts, on_device(): lax.all_to_all(lax.all_to_all(contracted, 'row', split_axis=1, concat_axi...  5.39 us
    all_to_all x1, starting transfers between devices, on_device(): lax.all_to_all(lax.all_to_all(contracted, 'row', split_axis=1, concat_axi...  5.07 us
  transfers between devices with their start and end apart: 3, of which 3 were waited for; matrix products, arithmetic and copies ran while one was open for 1% of the time, Pallas kernels for 0%

commit v1 on v0

v1 whole, which is shorter than its diff:
```python
import functools
import math

import jax
import jax.numpy as jnp
from jax import lax
from jax.experimental import pallas as pl
from jax.experimental.pallas import tpu as pltpu
from jax.sharding import PartitionSpec as P

MESH = pl.DeviceIdType.MESH
POWER = 7
LARGEST_T = 6.0
LARGEST_W = 0.109375


def coded(x, scale):
    x = x * scale
    x2 = x * x
    return (x2 * x2 * x2 * x).astype(jnp.bfloat16)


def decoded(y, scale):
    y = y.astype(jnp.float32)
    size = jnp.abs(y)
    root = jnp.exp2(jnp.log2(jnp.maximum(size, 1e-37)) * (1.0 / POWER)) * (1.0 / scale)
    root = jnp.where(size < 1e-37, 0.0, root)
    return jnp.where(y < 0, -root, root)


def kernel(
    rows, height, scale,
    w_ref, t_ref, out_ref,
    w_all, t_all, acc, enc, mirror, direct_out, direct_in,
    local_sem, w_swap, w_send, w_recv, t_send, t_recv, t_core_send, t_core_recv, m_send, m_recv, d_sem,
):
    r = lax.axis_index("row")
    c = lax.axis_index("col")
    hi, lo = c // 2, c % 2
    other = 1 - lo
    quads = rows // 2
    core, quad = r % 2, r // 2
    core_partner = r + 1 - 2 * core
    lo_partner = 2 * hi + other
    peers = rows * height
    me = r * height + hi
    occ = out_ref.shape[0]
    vd = out_ref.shape[1]

    barrier = pltpu.get_barrier_semaphore()

    def greet(d, carry):
        peer = lax.rem(me + d, peers)
        pl.semaphore_signal(barrier, inc=1, device_id=(peer // height, 2 * (peer % height) + lo), device_id_type=MESH)
        return carry

    lax.fori_loop(1, peers, greet, 0)
    pl.semaphore_signal(barrier, inc=1, device_id=(r, lo_partner), device_id_type=MESH)

    w_local = pltpu.make_async_copy(w_ref.at[lo], w_all.at[hi, lo], local_sem.at[0])
    t_local = pltpu.make_async_copy(t_ref, t_all.at[lo, r], local_sem.at[1])
    w_local.start()
    t_local.start()
    pl.semaphore_wait(barrier, peers)

    swap = pltpu.make_async_remote_copy(
        w_ref.at[other], w_all.at[hi, lo], w_swap.at[0], w_swap.at[1], device_id=(r, lo_partner), device_id_type=MESH)
    swap_in = pltpu.make_async_remote_copy(
        w_ref.at[other], w_all.at[hi, other], w_swap.at[0], w_swap.at[1], device_id=(r, lo_partner), device_id_type=MESH)

    def line_copy(way, step, sub, block):
        target = hi + 1 if way == 0 else hi - 1
        half = lo if sub == 0 else other
        source = w_ref.at[lo] if (step == 0 and sub == 0) else w_all.at[block, half]
        return pltpu.make_async_remote_copy(
            source, w_all.at[block, half], w_send.at[way, step, sub], w_recv.at[way, step, sub],
            device_id=(r, 2 * target + lo), device_id_type=MESH)

    def sends(way, step):
        if way == 0:
            return jnp.logical_and(hi + 1 < height, hi - step >= 0)
        return jnp.logical_and(hi >= 1, hi + step < height)

    def receives(way, step):
        return hi - 1 - step >= 0 if way == 0 else hi + 1 + step < height

    def send_line(way, step, sub):
        @pl.when(sends(way, step))
        def _():
            line_copy(way, step, sub, hi - step if way == 0 else hi + step).start()

    def wait_line(way, step, sub):
        @pl.when(receives(way, step))
        def _():
            line_copy(way, step, sub, hi - 1 - step if way == 0 else hi + 1 + step).wait_recv()

    def t_copy(which, source_r, target_r, target_c, send, recv):
        return pltpu.make_async_remote_copy(
            t_all.at[which, source_r], t_all.at[which, source_r], send, recv,
            device_id=(target_r, target_c), device_id_type=MESH)

    def t_row(k, d):
        which = lo if k == 0 else other
        target = 2 * lax.rem(quad + d, quads) + core
        source = t_ref if k == 0 else t_all.at[which, r]
        return pltpu.make_async_remote_copy(
            source, t_all.at[which, r], t_send.at[k, d], t_recv.at[k, d],
            device_id=(target, c), device_id_type=MESH)

    def t_row_in(k, d):
        which = lo if k == 0 else other
        source_r = 2 * lax.rem(quad + quads - d, quads) + core
        return source_r, t_copy(which, source_r, r, c, t_send.at[k, d], t_recv.at[k, d])

    def t_core(k, d, source_r, incoming=False):
        which = lo if k == 0 else other
        return t_copy(which, source_r, core_partner, c, t_core_send.at[k, d], t_core_recv.at[k, d])

    t_lo = pltpu.make_async_remote_copy(
        t_ref, t_all.at[lo, r], t_send.at[0, 0], t_recv.at[0, 0], device_id=(r, lo_partner), device_id_type=MESH)
    t_lo_in = t_copy(other, r, r, lo_partner, t_send.at[0, 0], t_recv.at[0, 0])

    swap.start()
    send_line(0, 0, 0)
    send_line(1, 0, 0)
    for d in range(1, quads):
        t_row(0, d).start()
    t_lo.start()
    t_local.wait()
    t_core(0, 0, r).start()
    w_local.wait()
    swap_in.wait_recv()
    send_line(0, 0, 1)
    send_line(1, 0, 1)

    def relay(step):
        for sub in range(2):
            for way in range(2):
                wait_line(way, step, sub)
                send_line(way, step + 1, sub)

    if height > 2:
        relay(0)
    for d in range(1, quads):
        source_r, copy = t_row_in(0, d)
        copy.wait_recv()
        t_core(0, d, source_r).start()
    t_lo_in.wait_recv()
    t_core(1, 0, r).start()
    for d in range(1, quads):
        t_row(1, d).start()
    for step in range(1, height - 2):
        relay(step)
    for d in range(1, quads):
        source_r, copy = t_row_in(1, d)
        copy.wait_recv()
        t_core(1, d, source_r).start()
    for k in range(2):
        for d in range(quads):
            source_r = 2 * lax.rem(quad + quads - d, quads) + 1 - core
            t_core(k, d, source_r).wait_recv()

    tile = min(256, t_ref.shape[0])
    tiles = t_ref.shape[0] // tile

    def multiply(block, first):
        weights = w_all.at[block]

        def body(n, carry):
            which, place = n // tiles, n % tiles
            at = pl.ds(pl.multiple_of(place * tile, tile), tile)
            left = t_all[which, block, at, :]
            right = jnp.concatenate([weights[0], weights[1]], axis=0)
            product = jnp.dot(left, right, preferred_element_type=jnp.float32)
            if first:
                acc[which, at, :] = product
            else:
                acc[which, at, :] += product
            return carry

        lax.fori_loop(0, 2 * tiles, body, 0)

    multiply(hi, True)
    for step in range(height - 1):
        for way in range(2):
            if step == height - 2:
                wait_line(way, step, 0)
                wait_line(way, step, 1)

            @pl.when(receives(way, step))
            def _():
                multiply(hi - 1 - step if way == 0 else hi + 1 + step, False)

    def code_mirror(n, carry):
        y, j = n // occ, n % occ
        at = pl.ds(pl.multiple_of(j * vd, vd), vd)
        values = coded(acc[y, at, :], scale)
        for z in range(height):
            enc[z, j, y] = values[:, z * vd:(z + 1) * vd]
        direct_out[y, at, :] = values
        return carry

    lax.fori_loop(0, 2 * occ, code_mirror, 0)

    own = pltpu.make_async_copy(enc.at[hi, r], mirror.at[r, hi], local_sem.at[0])
    own.start()

    def mirror_copy(d):
        peer = lax.rem(me + d, peers)
        pr, pz = peer // height, peer % height
        return pltpu.make_async_remote_copy(
            enc.at[pz, pr], mirror.at[r, hi], m_send.at[d], m_recv.at[d],
            device_id=(pr, 2 * pz + lo), device_id_type=MESH)

    def mirror_in(d):
        peer = lax.rem(me + peers - d, peers)
        pr, pz = peer // height, peer % height
        return pr, pz, pltpu.make_async_remote_copy(
            enc.at[pz, pr], mirror.at[pr, pz], m_send.at[d], m_recv.at[d],
            device_id=(pr, 2 * pz + lo), device_id_type=MESH)

    def send_mirror(d, carry):
        mirror_copy(d).start()
        return carry

    lax.fori_loop(1, peers, send_mirror, 0)
    direct = pltpu.make_async_remote_copy(
        direct_out.at[other], direct_in, d_sem.at[0], d_sem.at[1], device_id=(r, lo_partner), device_id_type=MESH)
    direct.start()

    swap.wait_send()
    t_lo.wait_send()
    for step in range(height - 1):
        for way in range(2):
            @pl.when(sends(way, step))
            def _():
                for sub in range(2):
                    line_copy(way, step, sub, hi - step if way == 0 else hi + step).wait_send()
    for k in range(2):
        for d in range(1, quads):
            t_row(k, d).wait_send()
        for d in range(quads):
            t_core(k, d, r).wait_send()

    own.wait()

    def wait_mirror(d, carry):
        mirror_in(d)[2].wait_recv()
        mirror_copy(d).wait_send()
        return carry

    direct.wait()
    lax.fori_loop(1, peers, wait_mirror, 0)

    def combine(j, carry):
        at = pl.ds(pl.multiple_of(j * vd, vd), vd)
        mine = acc[lo, at, :]
        theirs = decoded(direct_in[at, :], scale)
        for z in range(height):
            span = slice(z * vd, (z + 1) * vd)
            for y in range(2):
                here = jnp.where(lo == y, mine[:, span], theirs[:, span])
                there = decoded(mirror[j, z, y], scale)
                col = 2 * z + y
                out_ref[j, :, col * vd:(col + 1) * vd] = here + there.T
        return carry

    lax.fori_loop(0, occ, combine, 0)


def on_device(rows, cols, w_inter, t_panel, amplitudes, e_occ, e_vir):
    row_index = lax.axis_index("row")
    col_index = lax.axis_index("col")
    kw, occ_dev, vir_all = w_inter.shape
    vd, occ, kt = t_panel.shape
    height = cols // 2
    bound = LARGEST_T * LARGEST_W * kw * cols
    scale = 2.0 ** math.floor(119.0 / POWER - math.log2(bound))
    w_half = w_inter.reshape(kw, height, 2, vd).transpose(2, 0, 1, 3).reshape(2, kw, height * vd)
    t_rows = jnp.transpose(t_panel, (1, 0, 2)).reshape(occ * vd, kt)
    half = vir_all // 2
    dma = pltpu.SemaphoreType.DMA
    vmem = pl.BlockSpec(memory_space=pltpu.VMEM)
    residual = pl.pallas_call(
        functools.partial(kernel, rows, height, scale),
        out_shape=jax.ShapeDtypeStruct((occ, vd, vir_all), jnp.float32),
        in_specs=[vmem, vmem],
        out_specs=vmem,
        scratch_shapes=[
            pltpu.VMEM((height, 2, kw, half), jnp.bfloat16),
            pltpu.VMEM((2, rows, occ * vd, kt), jnp.bfloat16),
            pltpu.VMEM((2, occ * vd, half), jnp.float32),
            pltpu.VMEM((height, occ, 2, vd, vd), jnp.bfloat16),
            pltpu.VMEM((occ, height, 2, vd, vd), jnp.bfloat16),
            pltpu.VMEM((2, occ * vd, half), jnp.bfloat16),
            pltpu.VMEM((occ * vd, half), jnp.bfloat16),
            dma((2,)),
            dma((2,)),
            dma((2, height - 1, 2)),
            dma((2, height - 1, 2)),
            dma((2, rows // 2)),
            dma((2, rows // 2)),
            dma((2, rows // 2)),
            dma((2, rows // 2)),
            dma((rows * height,)),
            dma((rows * height,)),
            dma((2,)),
        ],
        compiler_params=pltpu.CompilerParams(
            collective_id=0, has_side_effects=True, vmem_limit_bytes=60 * 1024 * 1024),
        name="amplitude_residual",
    )(w_half, t_rows)
    residual = jnp.transpose(residual, (1, 0, 2))[:, :, None, :]
    occ_mine = lax.dynamic_slice_in_dim(e_occ, row_index * occ_dev, occ_dev)
    vir_mine = lax.dynamic_slice_in_dim(e_vir, col_index * vd, vd)
    gaps = (
        e_occ[None, :, None, None]
        + occ_mine[None, None, :, None]
        - vir_mine[:, None, None, None]
        - e_vir[None, None, None, :]
    )
    return amplitudes + residual / gaps


def solution(mesh):
    rows, cols = mesh.shape["row"], mesh.shape["col"]
    return jax.shard_map(
        functools.partial(on_device, rows, cols),
        mesh=mesh,
        in_specs=(
            P("col", "row", None),
            P("col", None, "row"),
            P("col", None, "row", None),
            P(),
            P(),
        ),
        out_specs=P("col", None, "row", None),
        check_vma=False,
    )
```

time: 249 us -> 102 us (0.41); the launches traced: 245 us -> 101 us
  waiting for transfers between devices: 173 us -> 0 us
  Pallas kernels: 0 us -> 85.9 us
  blocking collectives: 28.7 us -> 0 us
  between operations: 13.4 us -> 0.05 us
  matrix products: 6.44 us -> 0 us
  starting transfers between devices: 5.11 us -> 0 us
  local copies, waits for them, and re-layouts: 13.5 us -> 10.5 us
    all_gather x2 -> x0, waiting for transfers between devices: 127 us -> none  [the longest x1 98.8 us: on_device(): piece = lax.all_gather(w_inter, 'col', axis=0, tiled=True)]
    pallas_call x0 -> x1, Pallas kernels: none -> 85.9 us  [on_device(): pl.pallas_call(functools.partial(kernel, rows, height, scale), out_shape=...]
    all_to_all x1 -> x0, waiting for transfers between devices: 45.1 us -> none  [on_device(): lax.all_to_all(lax.all_to_all(contracted, 'row', split_axis=1, concat_axi...]
    all_to_all x1 -> x0, blocking collectives: 28.7 us -> none  [on_device(): lax.all_to_all(contracted, 'row', split_axis=1, concat_axis=2, tiled=True)]
    all_to_all x3 -> x0, local copies, waits for them, and re-layouts: 7.19 us -> none  [the longest x2 5.39 us: on_device(): lax.all_to_all(lax.all_to_all(contracted, 'row', split_axis=1, concat_axi...]
    dot_general x1 -> x0, matrix products: 6.44 us -> none  [on_device(): jnp.dot(t_matrix, piece.reshape(row_count, occ_dev * vir_all), preferred_...]
    all_to_all x1 -> x0, starting transfers between devices: 5.07 us -> none  [on_device(): lax.all_to_all(lax.all_to_all(contracted, 'row', split_axis=1, concat_axi...]
    reshape x0 -> x3, local copies, waits for them, and re-layouts: none -> 4.01 us  [on_device(): w_inter.reshape(kw, height, 2, vd).transpose(2, 0, 1, 3)]
  transfers between devices with their start and end apart: 3 -> 0, of which waited for: 3 -> 0; matrix products, arithmetic and copies ran while one was open for 1% -> 0% of each run, Pallas kernels for 0% -> 0%
where the time goes in v1:
time: 102 us; the launch traced here: 101 us
  Pallas kernels  85.9 us (84%)
  local copies, waits for them, and re-layouts  10.5 us (10%)
  other arithmetic  4.27 us (4%)
    pallas_call x1, Pallas kernels, on_device(): pl.pallas_call(functools.partial(kernel, rows, height, scale), out_shape=...  85.9 us
    reshape x3, local copies, waits for them, and re-layouts, on_device(): w_inter.reshape(kw, height, 2, vd).transpose(2, 0, 1, 3)  4.01 us
    add x1, local copies, waits for them, and re-layouts, on_device(): return amplitudes + residual / gaps  3.48 us
    add x1, other arithmetic, on_device(): return amplitudes + residual / gaps  2.9 us

profile of v1, /device:TPU:11, one launch (start us, length us, event | category | flops | bytes accessed | tf_op | source)
XLA Modules:
  0.0 100.7 jit_solution(10267881462219143097)
XLA Ops:
  0.0 1.2 %dynamic_slice.6 = f32[1]{0:T(128)} dynamic-slice(f32[4]{0:T(128)} %param.8, s32[]{:T(128)S(6)} %select_n.6), dynamic_slice_sizes={1} | dynamic-slice | bytes 12 | tf_op jit(solution)/shard_map/dynamic_slice | solution.py:314
  1.2 1.3 %broadcast_add_fusion = f32[4]{0:T(128)S(1)} fusion(f32[4]{0:T(128)} %param.8, f32[]{:T(128)} %bitcast.4), kind=kLoop, calls=%fused_computation.4 | loop fusion | flops 4 | bytes 36 | tf_op jit(solution)/shard_map/add | solution.py:317
  2.5 0.8 dynamic_slice.7
  3.3 0.1 broadcast_subtract_fusion
  3.4 0.0 copy-start.1
  3.4 2.6 %reshape.52 = bf16[384,4,2,128]{3,2,1,0:T(2,128)(2,1)S(1)} reshape(bf16[384,1,1024]{2,0,1:T(8,128)(2,1)} %param.5) | data formatting | bytes 1572864 | tf_op jit(solution)/shard_map/reshape | solution.py:279
  6.0 0.2 copy.12
  6.2 1.2 %reshape.53.w_ref = bf16[2,384,512]{2,1,0:T(8,128)(2,1)} reshape(bf16[2,384,4,128]{3,2,1,0:T(4,128)(2,1)S(1)} %bitcast.15) | data formatting | bytes 1572864 | tf_op jit(solution)/shard_map/reshape | solution.py:279
  7.4 0.0 copy-done.1
  7.4 1.0 copy.7
  8.4 0.0 copy-start
  8.4 0.0 copy-start.2
  8.4 85.9 %amplitude_residual.1 = f32[4,128,1024]{2,1,0:T(8,128)} custom-call(bf16[2,384,512]{2,1,0:T(8,128)(2,1)} %reshape.53.w_ref, bf16[512,768]{1,0:T(8,128)(2,1)} %bitcast.14), custom_call_target="tpu_custom_call" | custom-call | tf_op jit(solution)/shard_map/amplitude_residual/pallas_call | solution.py:284
  94.3 0.0 copy-done
  94.3 0.0 copy-done.2
  94.3 2.9 %bitcast_add_fusion = f32[128,4,1,1024]{3,0,1,2:T(8,128)S(1)} fusion(f32[4,128,1024]{2,1,0:T(8,128)} %amplitude_residual.1, f32[128,4,1,1024]{3,2,1,0:T(1,128)S(1)} %copy-done, f32[1024]{0:T(1024)S(1)} %copy-done.2, f32[128,4]{0,1:T(4,128)S(1)} %broadcast_subtract_fusion), kind=kLoop, calls=%fused_computation | loop fusion | flops 1572864 | bytes 6297600 | tf_op jit(solution)/shard_map/add | solution.py:322
  97.2 3.5 %copy.9 = f32[128,4,1,1024]{3,2,1,0:T(1,128)} copy(f32[128,4,1,1024]{3,0,1,2:T(8,128)S(1)} %bitcast_add_fusion) | data formatting | bytes 4194304 | tf_op jit(solution)/shard_map/add | solution.py:322
Async XLA Ops:
  3.4 4.0 %copy-start.1 = (bf16[128,4,768]{2,1,0:T(4,128)(2,1)S(1)}, bf16[128,4,768]{2,1,0:T(4,128)(2,1)}, u32[]{:S(2)}) copy-start(bf16[128,4,768]{2,1,0:T(4,128)(2,1)} %param.6) | copy-start | bytes 2359300
  8.4 85.9 %copy-start = (f32[128,4,1,1024]{3,2,1,0:T(1,128)S(1)}, f32[128,4,1,1024]{3,2,1,0:T(1,128)}, u32[]{:S(2)}) copy-start(f32[128,4,1,1024]{3,2,1,0:T(1,128)} %param.7) | copy-start | bytes 6291460
  8.4 85.9 %copy-start.2 = (f32[1024]{0:T(1024)S(1)}, f32[1024]{0:T(1024)}, u32[]{:S(2)}) copy-start(f32[1024]{0:T(1024)} %param.9) | copy-start | bytes 12292

commit v2 on v1

--- a/solution.py
+++ b/solution.py
@@ -30,9 +30,9 @@
 
 def kernel(
     rows, height, scale,
-    w_ref, t_ref, out_ref,
-    w_all, t_all, acc, enc, mirror, direct_out, direct_in,
-    local_sem, w_swap, w_send, w_recv, t_send, t_recv, t_core_send, t_core_recv, m_send, m_recv, d_sem,
+    w_ref, t_ref, eo_ref, evb_ref, eva_ref, out_ref,
+    w_all, w_out, t_all, acc, enc, mirror, direct_out, direct_in, theirs,
+    w_sem, local_sem, w_swap, w_send, w_recv, t_send, t_recv, t_core_send, t_core_recv, m_send, m_recv, d_sem,
 ):
     r = lax.axis_index("row")
     c = lax.axis_index("col")
@@ -44,8 +44,27 @@
     lo_partner = 2 * hi + other
     peers = rows * height
     me = r * height + hi
-    occ = out_ref.shape[0]
-    vd = out_ref.shape[1]
+    vd = evb_ref.shape[1]
+    occ = eo_ref.shape[0]
+    kw = w_ref.shape[0]
+    half = height * vd
+    width = vd if vd % 128 == 0 else half
+
+    def w_columns(buffer, slot, parity):
+        copies = []
+        for n in range(half // width):
+            start = pl.multiple_of((2 * n + parity) * width, 128)
+            copies.append(pltpu.make_async_copy(
+                w_ref.at[:, pl.ds(start, width)], buffer.at[:, n * width:(n + 1) * width], w_sem.at[slot, n]))
+        return copies
+
+    def w_block(block, part):
+        return w_all.at[block, pl.ds(pl.multiple_of(part * kw, kw), kw), :]
+
+    w_own = w_columns(w_block(hi, lo), 0, lo)
+    w_swap_out = w_columns(w_out, 1, other)
+    for copy in w_swap_out + w_own:
+        copy.start()
 
     barrier = pltpu.get_barrier_semaphore()
 
@@ -57,23 +76,22 @@
     lax.fori_loop(1, peers, greet, 0)
     pl.semaphore_signal(barrier, inc=1, device_id=(r, lo_partner), device_id_type=MESH)
 
-    w_local = pltpu.make_async_copy(w_ref.at[lo], w_all.at[hi, lo], local_sem.at[0])
     t_local = pltpu.make_async_copy(t_ref, t_all.at[lo, r], local_sem.at[1])
-    w_local.start()
     t_local.start()
+    for copy in w_swap_out + w_own:
+        copy.wait()
     pl.semaphore_wait(barrier, peers)
 
     swap = pltpu.make_async_remote_copy(
-        w_ref.at[other], w_all.at[hi, lo], w_swap.at[0], w_swap.at[1], device_id=(r, lo_partner), device_id_type=MESH)
+        w_out, w_block(hi, lo), w_swap.at[0], w_swap.at[1], device_id=(r, lo_partner), device_id_type=MESH)
     swap_in = pltpu.make_async_remote_copy(
-        w_ref.at[other], w_all.at[hi, other], w_swap.at[0], w_swap.at[1], device_id=(r, lo_partner), device_id_type=MESH)
+        w_out, w_block(hi, other), w_swap.at[0], w_swap.at[1], device_id=(r, lo_partner), device_id_type=MESH)
 
     def line_copy(way, step, sub, block):
         target = hi + 1 if way == 0 else hi - 1
-        half = lo if sub == 0 else other
-        source = w_ref.at[lo] if (step == 0 and sub == 0) else w_all.at[block, half]
-        return pltpu.make_async_remote_copy(
-            source, w_all.at[block, half], w_send.at[way, step, sub], w_recv.at[way, step, sub],
+        part = lo if sub == 0 else other
+        return pltpu.make_async_remote_copy(
+            w_block(block, part), w_block(block, part), w_send.at[way, step, sub], w_recv.at[way, step, sub],
             device_id=(r, 2 * target + lo), device_id_type=MESH)
 
     def sends(way, step):
@@ -128,7 +146,6 @@
     t_lo.start()
     t_local.wait()
     t_core(0, 0, r).start()
-    w_local.wait()
     swap_in.wait_recv()
     send_line(0, 0, 1)
     send_line(1, 0, 1)
@@ -164,14 +181,11 @@
     tiles = t_ref.shape[0] // tile
 
     def multiply(block, first):
-        weights = w_all.at[block]
-
         def body(n, carry):
             which, place = n // tiles, n % tiles
             at = pl.ds(pl.multiple_of(place * tile, tile), tile)
             left = t_all[which, block, at, :]
-            right = jnp.concatenate([weights[0], weights[1]], axis=0)
-            product = jnp.dot(left, right, preferred_element_type=jnp.float32)
+            product = jnp.dot(left, w_all[block], preferred_element_type=jnp.float32)
             if first:
                 acc[which, at, :] = product
             else:
@@ -191,39 +205,39 @@
             def _():
                 multiply(hi - 1 - step if way == 0 else hi + 1 + step, False)
 
-    def code_mirror(n, carry):
-        y, j = n // occ, n % occ
+    def mirror_copy(pr, pz):
+        return pltpu.make_async_remote_copy(
+            enc.at[pz, pr], mirror.at[r, hi], m_send.at[pr, pz], m_recv.at[r, hi],
+            device_id=(pr, 2 * pz + lo), device_id_type=MESH)
+
+    def mirror_in(pr, pz):
+        return pltpu.make_async_remote_copy(
+            enc.at[pz, pr], mirror.at[pr, pz], m_send.at[pr, pz], m_recv.at[pr, pz],
+            device_id=(pr, 2 * pz + lo), device_id_type=MESH)
+
+    def elsewhere(pr, pz):
+        return jnp.logical_or(pr != r, pz != hi)
+
+    own = pltpu.make_async_copy(enc.at[hi, r], mirror.at[r, hi], local_sem.at[0])
+
+    def send_mirror(n, carry):
+        j = lax.rem(r + n + 1, occ)
         at = pl.ds(pl.multiple_of(j * vd, vd), vd)
-        values = coded(acc[y, at, :], scale)
-        for z in range(height):
-            enc[z, j, y] = values[:, z * vd:(z + 1) * vd]
-        direct_out[y, at, :] = values
+        for y in range(2):
+            values = coded(acc[y, at, :], scale)
+            for z in range(height):
+                enc[z, j, y] = values[:, z * vd:(z + 1) * vd]
+            direct_out[y, at, :] = values
+        for step in range(height):
+            z = jnp.where(2 * hi < height, height - 1 - step, step)
+
+            @pl.when(elsewhere(j, z))
+            def _():
+                mirror_copy(j, z).start()
         return carry
 
-    lax.fori_loop(0, 2 * occ, code_mirror, 0)
-
-    own = pltpu.make_async_copy(enc.at[hi, r], mirror.at[r, hi], local_sem.at[0])
+    lax.fori_loop(0, occ, send_mirror, 0)
     own.start()
-
-    def mirror_copy(d):
-        peer = lax.rem(me + d, peers)
-        pr, pz = peer // height, peer % height
-        return pltpu.make_async_remote_copy(
-            enc.at[pz, pr], mirror.at[r, hi], m_send.at[d], m_recv.at[d],
-            device_id=(pr, 2 * pz + lo), device_id_type=MESH)
-
-    def mirror_in(d):
-        peer = lax.rem(me + peers - d, peers)
-        pr, pz = peer // height, peer % height
-        return pr, pz, pltpu.make_async_remote_copy(
-            enc.at[pz, pr], mirror.at[pr, pz], m_send.at[d], m_recv.at[d],
-            device_id=(pr, 2 * pz + lo), device_id_type=MESH)
-
-    def send_mirror(d, carry):
-        mirror_copy(d).start()
-        return carry
-
-    lax.fori_loop(1, peers, send_mirror, 0)
     direct = pltpu.make_async_remote_copy(
         direct_out.at[other], direct_in, d_sem.at[0], d_sem.at[1], device_id=(r, lo_partner), device_id_type=MESH)
     direct.start()
@@ -243,57 +257,102 @@
             t_core(k, d, r).wait_send()
 
     own.wait()
-
-    def wait_mirror(d, carry):
-        mirror_in(d)[2].wait_recv()
-        mirror_copy(d).wait_send()
+    direct.wait()
+
+    def decode_direct(j, carry):
+        at = pl.ds(pl.multiple_of(j * vd, vd), vd)
+        theirs[at, :] = decoded(direct_in[at, :], scale)
         return carry
 
-    direct.wait()
-    lax.fori_loop(1, peers, wait_mirror, 0)
-
-    def combine(j, carry):
+    lax.fori_loop(0, occ, decode_direct, 0)
+    group = max(128 // vd, 1)
+    lanes = group * vd
+    lines = 2 * half // lanes
+    vir_mine = jnp.broadcast_to(evb_ref[pl.ds(c, 1), :], (lanes, vd)).T
+
+    def wait_mirror(pr, pz):
+        @pl.when(elsewhere(pr, pz))
+        def _():
+            mirror_in(pr, pz).wait_recv()
+
+    def combine(n, carry):
+        j = lax.rem(n, occ)
         at = pl.ds(pl.multiple_of(j * vd, vd), vd)
-        mine = acc[lo, at, :]
-        theirs = decoded(direct_in[at, :], scale)
-        for z in range(height):
-            span = slice(z * vd, (z + 1) * vd)
-            for y in range(2):
-                here = jnp.where(lo == y, mine[:, span], theirs[:, span])
-                there = decoded(mirror[j, z, y], scale)
-                col = 2 * z + y
-                out_ref[j, :, col * vd:(col + 1) * vd] = here + there.T
+        line = n // occ
+
+        def finish(first_z, count):
+            for z in range(first_z, first_z + count):
+                wait_mirror(j, z)
+            blocks = []
+            for z in range(first_z, first_z + count):
+                span = slice(z * vd, (z + 1) * vd)
+                for y in range(2):
+                    here = jnp.where(lo == y, acc[lo, at, span], theirs[at, span])
+                    blocks.append(here + decoded(mirror[j, z, y], scale).T)
+            for start in range(0, len(blocks), group):
+                piece = blocks[start:start + group]
+                value = piece[0] if group == 1 else jnp.concatenate(piece, axis=1)
+                row = (2 * first_z + start) // group
+                gaps = (eo_ref[j] + eo_ref[r]) - vir_mine - eva_ref[row:row + 1, :]
+                out_ref[pl.ds(j * lines + row, vd, stride=occ * lines), :] = value / gaps
+
+        count = max(group // 2, 1)
+        for place in range(height // count):
+            @pl.when(line == place)
+            def _():
+                finish(place * count, count)
         return carry
 
-    lax.fori_loop(0, occ, combine, 0)
+    count = max(group // 2, 1)
+    places = height // count
+    here_place = hi // count
+
+    def ordered(n, carry):
+        place = lax.rem(here_place + n // occ, places)
+        return combine(place * occ + lax.rem(r + n, occ), carry)
+
+    lax.fori_loop(0, places * occ, ordered, 0)
+
+    for pr in range(rows):
+        for pz in range(height):
+            @pl.when(elsewhere(pr, pz))
+            def _():
+                mirror_copy(pr, pz).wait_send()
 
 
 def on_device(rows, cols, w_inter, t_panel, amplitudes, e_occ, e_vir):
-    row_index = lax.axis_index("row")
-    col_index = lax.axis_index("col")
     kw, occ_dev, vir_all = w_inter.shape
     vd, occ, kt = t_panel.shape
     height = cols // 2
     bound = LARGEST_T * LARGEST_W * kw * cols
     scale = 2.0 ** math.floor(119.0 / POWER - math.log2(bound))
-    w_half = w_inter.reshape(kw, height, 2, vd).transpose(2, 0, 1, 3).reshape(2, kw, height * vd)
+    w_matrix = w_inter.reshape(kw, vir_all)
+    width = vd
+    if vd % 128:
+        w_matrix = w_matrix.reshape(kw, height, 2, vd).transpose(0, 2, 1, 3).reshape(kw, vir_all)
+        width = height * vd
     t_rows = jnp.transpose(t_panel, (1, 0, 2)).reshape(occ * vd, kt)
     half = vir_all // 2
     dma = pltpu.SemaphoreType.DMA
     vmem = pl.BlockSpec(memory_space=pltpu.VMEM)
-    residual = pl.pallas_call(
+    lanes = max(128, vd)
+    smem = pl.BlockSpec(memory_space=pltpu.SMEM)
+    update = pl.pallas_call(
         functools.partial(kernel, rows, height, scale),
-        out_shape=jax.ShapeDtypeStruct((occ, vd, vir_all), jnp.float32),
-        in_specs=[vmem, vmem],
+        out_shape=jax.ShapeDtypeStruct((vd * occ * vir_all // lanes, lanes), jnp.float32),
+        in_specs=[pl.BlockSpec(memory_space=pl.ANY), vmem, smem, vmem, vmem],
         out_specs=vmem,
         scratch_shapes=[
-            pltpu.VMEM((height, 2, kw, half), jnp.bfloat16),
+            pltpu.VMEM((height, 2 * kw, half), jnp.bfloat16),
+            pltpu.VMEM((kw, half), jnp.bfloat16),
             pltpu.VMEM((2, rows, occ * vd, kt), jnp.bfloat16),
             pltpu.VMEM((2, occ * vd, half), jnp.float32),
             pltpu.VMEM((height, occ, 2, vd, vd), jnp.bfloat16),
             pltpu.VMEM((occ, height, 2, vd, vd), jnp.bfloat16),
             pltpu.VMEM((2, occ * vd, half), jnp.bfloat16),
             pltpu.VMEM((occ * vd, half), jnp.bfloat16),
+            pltpu.VMEM((occ * vd, half), jnp.float32),
+            dma((2, half // width)),
             dma((2,)),
             dma((2,)),
             dma((2, height - 1, 2)),
@@ -302,24 +361,15 @@
             dma((2, rows // 2)),
             dma((2, rows // 2)),
             dma((2, rows // 2)),
-            dma((rows * height,)),
-            dma((rows * height,)),
+            dma((rows, height)),
+            dma((rows, height)),
             dma((2,)),
         ],
         compiler_params=pltpu.CompilerParams(
             collective_id=0, has_side_effects=True, vmem_limit_bytes=60 * 1024 * 1024),
         name="amplitude_residual",
-    )(w_half, t_rows)
-    residual = jnp.transpose(residual, (1, 0, 2))[:, :, None, :]
-    occ_mine = lax.dynamic_slice_in_dim(e_occ, row_index * occ_dev, occ_dev)
-    vir_mine = lax.dynamic_slice_in_dim(e_vir, col_index * vd, vd)
-    gaps = (
-        e_occ[None, :, None, None]
-        + occ_mine[None, None, :, None]
-        - vir_mine[:, None, None, None]
-        - e_vir[None, None, None, :]
-    )
-    return amplitudes + residual / gaps
+    )(w_matrix, t_rows, e_occ, e_vir.reshape(cols, vd), e_vir.reshape(vir_all // lanes, lanes))
+    return amplitudes + update.reshape(amplitudes.shape)
 
 
 def solution(mesh):

time: 102 us -> 95.8 us (0.939); the launches traced: 101 us -> 95.6 us
  local copies, waits for them, and re-layouts: 10.5 us -> 2.09 us
  other arithmetic: 4.27 us -> 6.56 us
    reshape x3 -> x0, local copies, waits for them, and re-layouts: 4.01 us -> none  [on_device(): w_inter.reshape(kw, height, 2, vd).transpose(2, 0, 1, 3)]
    add x1 -> x0, local copies, waits for them, and re-layouts: 3.48 us -> none  [on_device(): return amplitudes + residual / gaps]
    add x2 -> x1, other arithmetic: 4.2 us -> 6.56 us  [on_device(): return amplitudes + update.reshape(amplitudes.shape)]
    dynamic_slice x2 -> x0, local copies, waits for them, and re-layouts: 2 us -> none  [the longest x1 1.24 us: on_device(): occ_mine = lax.dynamic_slice_in_dim(e_occ, row_index * occ_dev, occ_dev)]
    transpose x1, local copies, waits for them, and re-layouts: 0.98 us -> 2.09 us  [on_device(): t_rows = jnp.transpose(t_panel, (1, 0, 2)).reshape(occ * vd, kt)]
where the time goes in v2:
time: 95.8 us; the launch traced here: 95.6 us
  Pallas kernels  86.9 us (91%)
  other arithmetic  6.56 us (7%)
  local copies, waits for them, and re-layouts  2.09 us (2%)
    pallas_call x1, Pallas kernels, on_device(): pl.pallas_call(functools.partial(kernel, rows, height, scale), out_shape=...  86.9 us
    add x1, other arithmetic, on_device(): return amplitudes + update.reshape(amplitudes.shape)  6.56 us
    transpose x1, local copies, waits for them, and re-layouts, on_device(): t_rows = jnp.transpose(t_panel, (1, 0, 2)).reshape(occ * vd, kt)  2.09 us

profile of v2, /device:TPU:11, one launch (start us, length us, event | category | flops | bytes accessed | tf_op | source)
XLA Modules:
  0.0 95.6 jit_solution(2127955835135923023)
XLA Ops:
  0.0 2.1 %copy.6 = bf16[4,128,768]{2,1,0:T(8,128)(2,1)} copy(bf16[4,128,768]{2,0,1:T(4,128)(2,1)} %bitcast.7) | data formatting | bytes 1572864 | tf_op jit(solution)/shard_map/transpose | solution.py:334
  2.1 0.0 copy-start
  2.1 86.9 %amplitude_residual.1 = f32[4096,128]{1,0:T(8,128)} custom-call(bf16[384,1024]{1,0:T(8,128)(2,1)} %bitcast.8, bf16[512,768]{1,0:T(8,128)(2,1)} %bitcast.6, f32[4]{0:T(128)} %eo_ref.1, f32[8,128]{1,0:T(8,128)} %bitcast.9, f32[8,128]{1,0:T(8,128)} %bitcast.10), custom_call_target="tpu_custom_call" | custom-call | tf_op jit(solution)/shard_map/amplitude_residual/pallas_call | solution.py:340
  89.0 0.0 copy-done
  89.0 6.6 %add.3 = f32[128,4,1,1024]{3,2,1,0:T(1,128)} add(f32[128,4,1,1024]{3,2,1,0:T(1,128)S(1)} %copy-done, f32[128,4,1,1024]{3,2,1,0:T(1,128)} %bitcast.5) | non-fusion elementwise | flops 524288 | bytes 6291456 | tf_op jit(solution)/shard_map/add | solution.py:372
Async XLA Ops:
  2.1 86.9 %copy-start = (f32[128,4,1,1024]{3,2,1,0:T(1,128)S(1)}, f32[128,4,1,1024]{3,2,1,0:T(1,128)}, u32[]{:S(2)}) copy-start(f32[128,4,1,1024]{3,2,1,0:T(1,128)} %param.7) | copy-start | bytes 6291460

commit v3 on v2

--- a/solution.py
+++ b/solution.py
@@ -369,7 +369,7 @@
             collective_id=0, has_side_effects=True, vmem_limit_bytes=60 * 1024 * 1024),
         name="amplitude_residual",
     )(w_matrix, t_rows, e_occ, e_vir.reshape(cols, vd), e_vir.reshape(vir_all // lanes, lanes))
-    return amplitudes + update.reshape(amplitudes.shape)
+    return (lax.optimization_barrier(amplitudes.reshape(update.shape)) + update).reshape(amplitudes.shape)
 
 
 def solution(mesh):

time: 95.8 us -> 92.4 us (0.965)
  other arithmetic: 6.56 us -> 3.12 us
    add x1, other arithmetic: 6.56 us -> 3.12 us  [on_device(): lax.optimization_barrier(amplitudes.reshape(update.shape)) + update]
where the time goes in v3:
time: 92.4 us; the launch traced here: 92.1 us
  Pallas kernels  86.9 us (94%)
  other arithmetic  3.12 us (3%)
  local copies, waits for them, and re-layouts  2.09 us (2%)
    pallas_call x1, Pallas kernels, on_device(): pl.pallas_call(functools.partial(kernel, rows, height, scale), out_shape=...  86.9 us
    add x1, other arithmetic, on_device(): lax.optimization_barrier(amplitudes.reshape(update.shape)) + update  3.12 us
    transpose x1, local copies, waits for them, and re-layouts, on_device(): t_rows = jnp.transpose(t_panel, (1, 0, 2)).reshape(occ * vd, kt)  2.09 us

profile of v3, /device:TPU:11, one launch (start us, length us, event | category | flops | bytes accessed | tf_op | source)
XLA Modules:
  0.0 92.1 jit_solution(16832979097127265540)
XLA Ops:
  0.0 2.1 %copy.6 = bf16[4,128,768]{2,1,0:T(8,128)(2,1)} copy(bf16[4,128,768]{2,0,1:T(4,128)(2,1)} %bitcast.8) | data formatting | bytes 1572864 | tf_op jit(solution)/shard_map/transpose | solution.py:334
  2.1 0.0 copy-start
  2.1 86.9 %amplitude_residual.1 = f32[4096,128]{1,0:T(8,128)} custom-call(bf16[384,1024]{1,0:T(8,128)(2,1)} %bitcast.9, bf16[512,768]{1,0:T(8,128)(2,1)} %bitcast.6, f32[4]{0:T(128)} %eo_ref.1, f32[8,128]{1,0:T(8,128)} %bitcast.10, f32[8,128]{1,0:T(8,128)} %bitcast.11), custom_call_target="tpu_custom_call" | custom-call | tf_op jit(solution)/shard_map/amplitude_residual/pallas_call | solution.py:340
  89.0 0.0 copy-done
  89.0 3.1 %add.3 = f32[4096,128]{1,0:T(8,128)} add(f32[4096,128]{1,0:T(8,128)S(1)} %bitcast.7, f32[4096,128]{1,0:T(8,128)} %amplitude_residual.1) | non-fusion elementwise | flops 524288 | bytes 6291456 | tf_op jit(solution)/shard_map/add | solution.py:372
Async XLA Ops:
  2.1 86.9 %copy-start = (f32[128,4,1,1024]{3,2,1,0:T(1,128)S(1)}, f32[128,4,1,1024]{3,2,1,0:T(1,128)}, u32[]{:S(2)}) copy-start(f32[128,4,1,1024]{3,2,1,0:T(1,128)} %param.7) | copy-start | bytes 6291460
